TPU v7x, 128 devices: a whole 4x4x4 slice. The times are simulated.
128 devices in a mesh: seq: 32 (over x, y, core), head: 4 (over z).
Axes of the slice: x: 4, y: 4, z: 4, core: 2. Of those that a mesh axis runs over, the one named last changes fastest.
Arguments:
- inputs: float32 [16384, 4096], P('seq', 'head'), may hold values from -6 to 6
- step_raw: float32 [64, 16384], P('head', 'seq'), may hold values from -4 to -2, as said below
- decay_rate: float32 [64], P('head'), may hold values from 0 to 1, as said below
- b_proj: float32 [16384, 128], P('seq'), may hold values from -0.5 to 0.5
- c_proj: float32 [16384, 128], P('seq'), may hold values from -0.5 to 0.5
- grad_out: float32 [16384, 4096], P('seq', 'head'), may hold values from -1.5 to 1.5
Outputs:
- grad_inputs: float32 [16384, 4096], P('seq', 'head')
- grad_step: float32 [64, 16384], P('head', 'seq')
- grad_b: float32 [16384, 128], P('seq')
- grad_c: float32 [16384, 128], P('seq')
Inputs may be any that keep to these rules, and one draw needn't show every extreme that they name: `step_raw`: softplus of each entry lies within 0.02 to 0.1. `decay_rate`: positive.
All inputs are finite; a program needn't handle non-finite values.
Results may differ from a plain program's by a relative error of at most 0.00022.
Values sent between devices are 32-bit elements; how exact they have to be, the bound alone decides.
A program may use at most 128 MiB of HBM per device.

v0:
```python
import jax
import jax.numpy as jnp
from jax import lax
from jax.experimental import pallas as pl
from jax.experimental.pallas import tpu as pltpu
from jax.sharding import PartitionSpec as P

HEAD_DIM = 64
STATE = 128
CHIPS = 16
TILE = 256
F32 = jnp.float32
BF16 = jnp.bfloat16
MESH = pl.DeviceIdType.MESH


def split2(a):
    high = a.astype(BF16)
    return high, (a - high.astype(F32)).astype(BF16)


def split3(a):
    first = a.astype(BF16)
    rest = a - first.astype(F32)
    second = rest.astype(BF16)
    return first, second, (rest - second.astype(F32)).astype(BF16)


def nn(a, b):
    return lax.dot_general(a, b, (((1,), (0,)), ((), ())), preferred_element_type=F32)


def nt(a, b):
    return lax.dot_general(a, b, (((1,), (1,)), ((), ())), preferred_element_type=F32)


def nn3(a, b):
    return nn(a[0], b[0]) + (nn(a[0], b[1]) + nn(a[1], b[0]))


def nt3(a, b):
    return nt(a[0], b[0]) + (nt(a[0], b[1]) + nt(a[1], b[0]))


def iota(shape, axis):
    return lax.broadcasted_iota(jnp.int32, shape, axis)


def kernel(
    x_ref, g_ref, raw_ref, rate_ref, b_ref, c_ref,
    gx_ref, graw_ref, gb_ref, gc_ref,
    ft, fac, xg, bt, ct, bs, cs, gm, amat, inner,
    v, dec, pv, pdec, vc, dc, r1, dr, r2, r3, ein, eout, es, edge,
    acc, z1, acc2, z2, red,
    pair_send, pair_recv, out_send, out_recv, dec_send, dec_recv,
    back_send, back_recv, z_send, z_recv,
):
    seq = lax.axis_index("seq")
    zed = lax.axis_index("head")
    chip = seq // 2
    core = seq % 2
    other = 1 - core
    partner = (2 * chip + other, zed)
    z_even = zed + 1 - 2 * (zed % 2)
    z_odd = (zed + 1 + 2 * ((zed + 1) % 2)) % 4
    length = x_ref.shape[0]
    heads = raw_ref.shape[0]
    half = length // 2
    first = (core == 0).astype(F32)
    second = 1.0 - first

    def peer(offset):
        return (chip + offset) % CHIPS

    barrier = pltpu.get_barrier_semaphore()
    for offset in range(1, CHIPS):
        pl.semaphore_signal(barrier, inc=1, device_id=(2 * peer(offset) + core, zed), device_id_type=MESH)
    for target in (partner, (seq, z_even), (seq, z_odd)):
        pl.semaphore_signal(barrier, inc=1, device_id=target, device_id_type=MESH)

    def lanes(tile):
        return pl.ds(pl.multiple_of(tile * TILE, TILE), TILE)

    raw = raw_ref[...]
    step = jnp.maximum(raw, 0.0) + jnp.log1p(jnp.exp(-jnp.abs(raw)))
    rate = rate_ref[...]
    log_decay = -rate * step
    rows = iota((length, length), 0)
    cols = iota((length, length), 1)
    upto = (rows <= cols).astype(F32).astype(BF16)
    sums = nn(jnp.concatenate(split3(log_decay), axis=0), upto)
    run = sums[:heads] + (sums[heads : 2 * heads] + sums[2 * heads :])
    before = run - log_decay
    factors = jnp.concatenate(
        [step * jnp.exp(-run), step * jnp.exp(before), jnp.exp(run), jnp.exp(-before)], axis=0
    )
    parts = [p.astype(F32) for p in split3(factors)]
    stack = jnp.concatenate(parts + [jnp.zeros_like(factors)], axis=0)
    ft[...] = jnp.transpose(stack).astype(BF16)
    for src, flat, turned in ((b_ref, bs, bt), (c_ref, cs, ct)):
        full = src[...]
        flat[0], flat[1] = split2(full)
        turned[0], turned[1] = split2(jnp.transpose(full))

    def pair(ref, *index):
        return ref[(0,) + index], ref[(1,) + index]

    def summarise(tile, block, offset):
        spread = ft[...]
        r = iota((TILE, TILE), 0)
        col = iota((TILE, TILE), 1)
        out = []
        for q in range(4):
            hot = ((r % 64) == q * 16 + tile * 4 + col // HEAD_DIM) & (r < 192)
            factor = nn(spread, hot.astype(F32).astype(BF16))
            fac[q, :, lanes(tile)] = factor
            source = x_ref if q < 2 else g_ref
            scaled = split2(factor * source[:, lanes(tile)])
            xg[q, 0, :, lanes(tile)] = scaled[0]
            xg[q, 1, :, lanes(tile)] = scaled[1]
            left = bt if q < 2 else ct
            out.append(nn3((left[0], left[1]), scaled))
            if q == 2:
                whole = factor[length - 1 : length, :]
        for flow, value in ((0, out[0] * whole), (1, out[3] * whole), (2, out[1]), (3, out[2])):
            v[block, :, flow, :, offset : offset + TILE] = value.reshape(CHIPS, 8, TILE)
        dec[block, :, offset : offset + TILE] = whole

    for j in range(2):
        summarise(2 * other + j, other, j * TILE)
    pl.semaphore_wait(barrier, CHIPS + 2)
    to_partner = [
        pltpu.make_async_remote_copy(v.at[other], pv, pair_send.at[0], pair_recv.at[0], device_id=partner, device_id_type=MESH),
        pltpu.make_async_remote_copy(dec.at[other], pdec, pair_send.at[1], pair_recv.at[1], device_id=partner, device_id_type=MESH),
    ]
    for copy in to_partner:
        copy.start()
    for j in range(2):
        summarise(2 * core + j, core, j * TILE)
    for copy in to_partner:
        copy.wait()

    own_decay = dec[core]
    mate_decay = pdec[...]
    ahead_own = first * mate_decay + second
    ahead_mate = first + second * own_decay
    behind_own = first + second * mate_decay
    behind_mate = first * own_decay + second
    dc[0] = own_decay * mate_decay

    def join(index):
        for flow in range(4):
            a, b = (ahead_own, ahead_mate) if flow < 2 else (behind_own, behind_mate)
            vc[index, flow] = a * v[core, index, flow] + b * pv[index, flow]

    outgoing = []
    for offset in range(1, CHIPS):
        there = peer(offset)
        join(there)
        device = (2 * there + core, zed)
        copy = pltpu.make_async_remote_copy(vc.at[there], r1.at[chip], out_send.at[offset], out_recv.at[offset], device_id=device, device_id_type=MESH)
        copy.start()
        outgoing.append(copy)
        copy = pltpu.make_async_remote_copy(dc.at[0], dr.at[chip], dec_send.at[offset], dec_recv.at[offset], device_id=device, device_id_type=MESH)
        copy.start()
        outgoing.append(copy)
    join(chip)
    r1[chip] = vc[chip]
    dr[chip] = dc[0]

    for r in range(2):
        row = slice(r * half, (r + 1) * half)
        forward = nt3((cs[0, row], cs[1, row]), (bs[0], bs[1]))
        backward = nt3((bs[0, row], bs[1, row]), (cs[0], cs[1]))
        i = iota((half, length), 0) + r * half
        j = iota((half, length), 1)
        for m, (value, keep) in enumerate(((forward, i >= j), (forward, i <= j), (backward, i <= j), (backward, i >= j))):
            gm[m, 0, row], gm[m, 1, row] = split2(jnp.where(keep, value, 0.0))

    def masked(m, source, tile, slot):
        lower = m % 2 == 0 if m < 2 else m == 3
        for r in range(2):
            row = slice(r * half, (r + 1) * half)
            if lower:
                depth = slice(0, (r + 1) * half)
            else:
                depth = slice(r * half, length)
            left = (gm[m, 0, row, depth], gm[m, 1, row, depth])
            right = (xg[source, 0, depth, lanes(tile)], xg[source, 1, depth, lanes(tile)])
            inner[slot, row, lanes(tile)] = nn3(left, right)

    def input_side(tile, carry):
        masked(2, 2, tile, 2)
        masked(3, 3, tile, 3)
        return carry

    lax.fori_loop(0, 4, input_side, 0)

    for copy in outgoing:
        copy.wait()
    ahead = [jnp.zeros((8, 2 * TILE), F32)] * 2
    for index in range(CHIPS):
        factor = dr[index]
        for flow in range(2):
            r2[index, flow] = ahead[flow]
            ahead[flow] = r1[index, flow] + factor * ahead[flow]
    behind = [jnp.zeros((8, 2 * TILE), F32)] * 2
    for index in reversed(range(CHIPS)):
        factor = dr[index]
        for flow in range(2):
            r2[index, 2 + flow] = behind[flow]
            behind[flow] = r1[index, 2 + flow] + factor * behind[flow]
    returning = []
    for offset in range(1, CHIPS):
        there = peer(offset)
        copy = pltpu.make_async_remote_copy(
            r2.at[there], r3.at[chip], back_send.at[offset], back_recv.at[offset], device_id=(2 * there + core, zed), device_id_type=MESH
        )
        copy.start()
        returning.append(copy)
    r3[chip] = r2[chip]

    amat[...] = jnp.zeros_like(amat)
    low = iota((half, half), 0) >= iota((half, half), 1)
    high = iota((half, half), 0) <= iota((half, half), 1)

    def output_side(tile, carry):
        masked(0, 0, tile, 0)
        masked(1, 1, tile, 1)
        upper = slice(0, half)
        under = slice(half, length)

        def block(a, row, b, col):
            return nt3(pair(xg.at[a], row, lanes(tile)), pair(xg.at[b], col, lanes(tile)))

        for part in (upper, under):
            amat[part, part] += jnp.where(low, block(2, part, 0, part), 0.0) + jnp.where(high, block(3, part, 1, part), 0.0)
        amat[under, upper] += block(2, under, 0, upper)
        amat[upper, under] += block(3, upper, 1, under)
        return carry

    lax.fori_loop(0, 4, output_side, 0)
    whole_a = amat[...]
    from_b = nn3(split2(whole_a), (bs[0], bs[1]))
    from_c = nn3(split2(jnp.transpose(whole_a)), (cs[0], cs[1]))
    for r in range(2):
        acc[r, 0] = from_c[r * half : (r + 1) * half]
        acc[r, 1] = from_b[r * half : (r + 1) * half]

    for copy in returning:
        copy.wait()

    def arrive(index, carry):
        for flow in range(4):
            value = r3[index, flow]
            if flow < 2:
                mine, mate = first, second
            else:
                mine, mate = second, first
            ein[core, index, flow] = (mine + mate * mate_decay) * value + mate * pv[index, flow]
            eout[index, flow] = (mate + mine * own_decay) * value + mine * v[core, index, flow]
        return carry

    lax.fori_loop(0, CHIPS, arrive, 0)
    give = pltpu.make_async_remote_copy(eout, ein.at[core], pair_send.at[2], pair_recv.at[2], device_id=partner, device_id_type=MESH)
    give.start()

    edge[...] = jnp.zeros_like(edge)

    def project(block, offset):
        tile = 2 * block + offset // TILE
        lane = slice(offset, offset + TILE)
        whole = dec[block, :, lane]
        state = [ein[block, :, flow, :, lane].reshape(STATE, TILE) for flow in range(4)]
        local_f = v[block, :, 0, :, lane].reshape(STATE, TILE)
        local_g = v[block, :, 2, :, lane].reshape(STATE, TILE)
        edge[0:1, lanes(tile)] = jnp.sum(state[3] * (local_f + whole * state[0]), axis=0, keepdims=True)
        edge[1:2, lanes(tile)] = jnp.sum(state[1] * (local_g + whole * state[2]), axis=0, keepdims=True)
        scaled = [split2(state[0]), split2(whole * state[2]), split2(whole * state[3]), split2(state[1])]
        for m in range(4):
            es[m, 0, :, lanes(tile)] = scaled[m][0]
            es[m, 1, :, lanes(tile)] = scaled[m][1]
        rows_of = [pair(xg.at[q], slice(None), lanes(tile)) for q in range(4)]
        read = nt3(rows_of[2], scaled[0]) + nt3(rows_of[3], scaled[1])
        write = nt3(rows_of[0], scaled[2]) + nt3(rows_of[1], scaled[3])
        for r in range(2):
            acc[r, 0] += write[r * half : (r + 1) * half]
            acc[r, 1] += read[r * half : (r + 1) * half]

    for j in range(2):
        project(core, j * TILE)
    give.wait()
    for j in range(2):
        project(other, j * TILE)

    def exchange(src, dst, first_sem, targets):
        copies = []
        for r in range(2):
            copies.append(pltpu.make_async_remote_copy(
                src.at[r], dst.at[r], z_send.at[first_sem + r], z_recv.at[first_sem + r], device_id=(seq, targets[r]), device_id_type=MESH
            ))
        for copy in copies:
            copy.start()
        return copies

    copies = exchange(acc, z1, 0, (z_even, z_odd))
    red[...] = jnp.zeros_like(red)

    def finish(tile, carry):
        lane = lanes(tile)
        full = slice(None)
        c_pair = (cs[0], cs[1])
        b_pair = (bs[0], bs[1])
        out_f = inner[0, :, lane] + nn3(c_pair, pair(es.at[0], full, lane))
        out_b = inner[1, :, lane] + nn3(c_pair, pair(es.at[1], full, lane))
        in_f = fac[0, :, lane] * (inner[2, :, lane] + nn3(b_pair, pair(es.at[2], full, lane)))
        in_b = fac[1, :, lane] * (inner[3, :, lane] + nn3(b_pair, pair(es.at[3], full, lane)))
        grad = in_f + in_b
        gx_ref[:, lane] = grad
        x = x_ref[:, lane]
        g = g_ref[:, lane]
        terms = (x * grad, g * (fac[2, :, lane] * out_f) - x * in_f, g * (fac[3, :, lane] * out_b) - x * in_b)
        r = iota((TILE, STATE), 0)
        col = iota((TILE, STATE), 1)
        total = red[...]
        for m in range(3):
            hot = (col == 16 * m + tile * 4 + r // HEAD_DIM).astype(F32).astype(BF16)
            a, b = split2(terms[m])
            total = total + (nn(a, hot) + nn(b, hot))
        red[...] = total
        return carry

    lax.fori_loop(0, 2, finish, 0)
    for copy in copies:
        copy.wait()
    acc2[...] = acc[...] + z1[...]
    copies = exchange(acc2, z2, 2, (z_odd, z_even))
    lax.fori_loop(2, 4, finish, 0)

    turned_red = jnp.transpose(red[...])
    direct = turned_red[:heads]
    hot = (iota((4 * TILE, STATE), 1) == iota((4 * TILE, STATE), 0) // HEAD_DIM).astype(F32).astype(BF16)
    edges = [nn(p, hot) for p in split3(edge[...])]
    edges = jnp.transpose(edges[0] + (edges[1] + edges[2]))
    after = (rows >= cols).astype(F32).astype(BF16)

    def running(value, matrix):
        out = nn(jnp.concatenate(split3(value), axis=0), matrix)
        return out[:heads] + (out[heads : 2 * heads] + out[2 * heads :])

    log_grad = running(turned_red[heads : 2 * heads], after) + edges[:heads, 0:1]
    log_grad = log_grad + running(turned_red[2 * heads : 3 * heads], upto) + edges[:heads, 1:2]
    graw_ref[...] = (direct / step - rate * log_grad) * jax.nn.sigmoid(raw)

    for copy in copies:
        copy.wait()
    for r in range(2):
        row = slice(r * half, (r + 1) * half)
        gb_ref[row] = acc2[r, 0] + z2[r, 0]
        gc_ref[row] = acc2[r, 1] + z2[r, 1]


def on_device(inputs, step_raw, decay_rate, b_proj, c_proj, grad_out):
    length, width = inputs.shape
    heads = step_raw.shape[0]
    vmem = pl.BlockSpec(memory_space=pltpu.VMEM)
    block = (CHIPS, 4, 8, width // 2)
    square = (length, length)
    half = length // 2
    dma = pltpu.SemaphoreType.DMA
    scratch = [
        pltpu.VMEM((length, 256), BF16),
        pltpu.VMEM((4, length, width), F32),
        pltpu.VMEM((4, 2, length, width), BF16),
        pltpu.VMEM((2, STATE, length), BF16),
        pltpu.VMEM((2, STATE, length), BF16),
        pltpu.VMEM((2, length, STATE), BF16),
        pltpu.VMEM((2, length, STATE), BF16),
        pltpu.VMEM((4, 2) + square, BF16),
        pltpu.VMEM(square, F32),
        pltpu.VMEM((4, length, width), F32),
        pltpu.VMEM((2,) + block, F32),
        pltpu.VMEM((2, 1, width // 2), F32),
        pltpu.VMEM(block, F32),
        pltpu.VMEM((1, width // 2), F32),
        pltpu.VMEM(block, F32),
        pltpu.VMEM((1, 1, width // 2), F32),
        pltpu.VMEM(block, F32),
        pltpu.VMEM((CHIPS, 1, width // 2), F32),
        pltpu.VMEM(block, F32),
        pltpu.VMEM(block, F32),
        pltpu.VMEM((2,) + block, F32),
        pltpu.VMEM(block, F32),
        pltpu.VMEM((4, 2, STATE, width), BF16),
        pltpu.VMEM((8, width), F32),
        pltpu.VMEM((2, 2, half, STATE), F32),
        pltpu.VMEM((2, 2, half, STATE), F32),
        pltpu.VMEM((2, 2, half, STATE), F32),
        pltpu.VMEM((2, 2, half, STATE), F32),
        pltpu.VMEM((length, STATE), F32),
        dma((3,)),
        dma((3,)),
        dma((CHIPS,)),
        dma((CHIPS,)),
        dma((CHIPS,)),
        dma((CHIPS,)),
        dma((CHIPS,)),
        dma((CHIPS,)),
        dma((4,)),
        dma((4,)),
    ]
    return pl.pallas_call(
        kernel,
        out_shape=(
            jax.ShapeDtypeStruct((length, width), F32),
            jax.ShapeDtypeStruct((heads, length), F32),
            jax.ShapeDtypeStruct((length, STATE), F32),
            jax.ShapeDtypeStruct((length, STATE), F32),
        ),
        in_specs=[vmem] * 6,
        out_specs=(vmem,) * 4,
        scratch_shapes=scratch,
        compiler_params=pltpu.CompilerParams(
            collective_id=0, has_side_effects=True, vmem_limit_bytes=67043328
        ),
        name="scan_backward",
    )(inputs, grad_out, step_raw, decay_rate.reshape(heads, 1), b_proj, c_proj)


def solution(mesh):
    return jax.shard_map(
        on_device,
        mesh=mesh,
        in_specs=(
            P("seq", "head"),
            P("head", "seq"),
            P("head"),
            P("seq", None),
            P("seq", None),
            P("seq", "head"),
        ),
        out_specs=(P("seq", "head"), P("head", "seq"), P("seq", None), P("seq", None)),
        check_vma=False,
    )
```

profile of v0, /device:TPU:1, one launch (start us, length us, event | category | flops | bytes accessed | tf_op | source)
XLA Modules:
  0.0 74.2 jit_solution(13112074586425085995)
XLA Ops:
  0.6 1.3 %copy.10.rate_ref = f32[16,1]{1,0:T(8,128)} copy(f32[16,1]{0,1:T(1,128)} %bitcast.1) | data formatting | bytes 128 | tf_op jit(solution)/shard_map/reshape | solution.py:427
  2.0 66.9 %scan_backward.1 = (f32[512,1024]{1,0:T(8,128)}, f32[16,512]{1,0:T(8,128)}, f32[512,128]{1,0:T(8,128)}, f32[512,128]{1,0:T(8,128)}) custom-call(f32[512,1024]{1,0:T(8,128)} %x_ref.1, f32[512,1024]{1,0:T(8,128)} %g_ref.1, f32[16,512]{1,0:T(8,128)} %raw_ref.1, f32[16,1]{1,0:T(8,128)} %copy.10.rate_ref, f32[512,128]{1,0:T(8,128)} %b_ref.1, f32[512,128]{1,0:T(8,128)} %c_ref.1), custom_call_target="tpu_custom_call" | custom-call | tf_op jit(solution)/shard_map/scan_backward/pallas_call | solution.py:412
  68.9 0.0 copy-start.2
  68.9 0.0 copy-start.1
  68.9 0.0 copy-start
  68.9 3.2 %copy.15 = f32[512,1024]{1,0:T(8,128)} copy(f32[512,1024]{1,0:T(8,128)} %get-tuple-element.8) | data formatting | bytes 4194304
  72.1 0.0 copy-done.2
  72.2 0.6 copy.16
  72.8 0.0 copy-done.1
  72.8 0.7 copy.17
  73.5 0.0 copy-done
  73.5 0.7 copy.18
Async XLA Ops:
  68.9 3.2 %copy-start.2 = (f32[16,512]{1,0:T(8,128)S(1)}, f32[16,512]{1,0:T(8,128)}, u32[]{:S(2)}) copy-start(f32[16,512]{1,0:T(8,128)} %get-tuple-element.9) | copy-start | bytes 98308
  68.9 3.9 %copy-start.1 = (f32[512,128]{1,0:T(8,128)S(1)}, f32[512,128]{1,0:T(8,128)}, u32[]{:S(2)}) copy-start(f32[512,128]{1,0:T(8,128)} %get-tuple-element.10) | copy-start | bytes 786436
  68.9 4.6 %copy-start = (f32[512,128]{1,0:T(8,128)S(1)}, f32[512,128]{1,0:T(8,128)}, u32[]{:S(2)}) copy-start(f32[512,128]{1,0:T(8,128)} %get-tuple-element.11) | copy-start | bytes 786436
where the time goes:
time: 74.8 us; the launch traced here: 74.2 us
  Pallas kernels  66.9 us (89%)
  local copies, waits for them, and re-layouts  6.58 us (9%)
    pallas_call x1, Pallas kernels, on_device(): pl.pallas_call(kernel, out_shape=(jax.ShapeDtypeStruct((length, width), F...  66.9 us
    unnamed x10, local copies, waits for them, and re-layouts  5.25 us

commit v1 on v0

v1 whole, which is shorter than its diff:
```python
import jax
import jax.numpy as jnp
from jax import lax
from jax.experimental import pallas as pl
from jax.experimental.pallas import tpu as pltpu
from jax.sharding import PartitionSpec as P

HEAD_DIM = 64
STATE = 128
CHIPS = 16
TILE = 256
F32 = jnp.float32
BF16 = jnp.bfloat16
MESH = pl.DeviceIdType.MESH


def split2(a):
    high = a.astype(BF16)
    return high, (a - high.astype(F32)).astype(BF16)


def split3(a):
    first = a.astype(BF16)
    rest = a - first.astype(F32)
    second = rest.astype(BF16)
    return first, second, (rest - second.astype(F32)).astype(BF16)


def nn(a, b):
    return lax.dot_general(a, b, (((1,), (0,)), ((), ())), preferred_element_type=F32)


def nt(a, b):
    return lax.dot_general(a, b, (((1,), (1,)), ((), ())), preferred_element_type=F32)


def nn3(a, b):
    return nn(a[0], b[0]) + (nn(a[0], b[1]) + nn(a[1], b[0]))


def nt3(a, b):
    return nt(a[0], b[0]) + (nt(a[0], b[1]) + nt(a[1], b[0]))


def iota(shape, axis):
    return lax.broadcasted_iota(jnp.int32, shape, axis)


OFFSETS = sorted(
    ((dx, dy) for dx in range(4) for dy in range(4) if dx or dy),
    key=lambda o: -(min(o[0], 4 - o[0]) + min(o[1], 4 - o[1])),
)


def kernel(
    x_hbm, g_hbm, raw_hbm, rate_hbm, b_hbm, c_hbm,
    gx_hbm, graw_ref, gb_ref, gc_ref,
    x_ref, g_ref, raw_ref, rate_ref, b_ref, c_ref, gx_ref,
    ft, fac, xg, bt, ct, bs, cs, gm, amat, inner,
    v, dec, pv, pdec, vc, dc, r1, dr, r2, r3, ein, eout, es, edge,
    acc, z1, acc2, z2, red,
    load_sem, store_sem, pair_send, pair_recv, out_send, out_recv, dec_send, dec_recv,
    back_send, back_recv, give_send, give_recv, z_send, z_recv,
):
    seq = lax.axis_index("seq")
    zed = lax.axis_index("head")
    chip = seq // 2
    core = seq % 2
    other = 1 - core
    chip_x = chip // 4
    chip_y = chip % 4
    partner = (2 * chip + other, zed)
    z_even = zed + 1 - 2 * (zed % 2)
    z_odd = (zed + 1 + 2 * ((zed + 1) % 2)) % 4
    length = x_ref.shape[0]
    heads = raw_ref.shape[0]
    half = length // 2
    first = (core == 0).astype(F32)
    second = 1.0 - first

    def peer(offset):
        dx, dy = OFFSETS[offset]
        return ((chip_x + dx) % 4) * 4 + (chip_y + dy) % 4

    def remote(src, dst, send, recv, device):
        return pltpu.make_async_remote_copy(src, dst, send, recv, device_id=device, device_id_type=MESH)

    barrier = pltpu.get_barrier_semaphore()
    for offset in range(CHIPS - 1):
        pl.semaphore_signal(barrier, inc=1, device_id=(2 * peer(offset) + core, zed), device_id_type=MESH)
    for target in (partner, (seq, z_even), (seq, z_odd)):
        pl.semaphore_signal(barrier, inc=1, device_id=target, device_id_type=MESH)
    loads = []
    for n, (src, dst) in enumerate((
        (raw_hbm, raw_ref), (rate_hbm, rate_ref), (c_hbm, c_ref), (g_hbm, g_ref), (b_hbm, b_ref), (x_hbm, x_ref)
    )):
        loads.append(pltpu.make_async_copy(src, dst, load_sem.at[n]))
        loads[-1].start()

    def lanes(tile):
        return pl.ds(pl.multiple_of(tile * TILE, TILE), TILE)

    rows = iota((length, length), 0)
    cols = iota((length, length), 1)
    upto = (rows <= cols).astype(F32).astype(BF16)
    loads[0].wait()
    loads[1].wait()
    raw = raw_ref[...]
    step = jnp.maximum(raw, 0.0) + jnp.log1p(jnp.exp(-jnp.abs(raw)))
    eye = iota((heads, heads), 0) == iota((heads, heads), 1)
    rate = jnp.sum(jnp.where(eye, rate_ref[...], 0.0), axis=1, keepdims=True)
    log_decay = -rate * step
    sums = nn(jnp.concatenate(split3(log_decay), axis=0), upto)
    run = sums[:heads] + (sums[heads : 2 * heads] + sums[2 * heads :])
    before = run - log_decay
    factors = jnp.concatenate(
        [step * jnp.exp(-run), step * jnp.exp(before), jnp.exp(run), jnp.exp(-before)], axis=0
    )
    parts = [p.astype(F32) for p in split3(factors)]
    stack = jnp.concatenate(parts + [jnp.zeros_like(factors)], axis=0)
    ft[...] = jnp.transpose(stack).astype(BF16)

    def turn(src, flat, turned):
        full = src[...]
        flat[0], flat[1] = split2(full)
        turned[0], turned[1] = split2(jnp.transpose(full))

    def pair(ref, *index):
        return ref[(0,) + index], ref[(1,) + index]

    def summarise(batch, tile, block, offset):
        spread = ft[...]
        r = iota((TILE, TILE), 0)
        col = iota((TILE, TILE), 1)
        source = (g_ref if batch == 0 else x_ref)[:, lanes(tile)]
        left = ct if batch == 0 else bt
        lane = slice(offset, offset + TILE)
        for q in ((2, 3) if batch == 0 else (1, 0)):
            hot = ((r % 64) == q * 16 + tile * 4 + col // HEAD_DIM) & (r < 192)
            factor = nn(spread, hot.astype(F32).astype(BF16))
            fac[q, :, lanes(tile)] = factor
            scaled = split2(factor * source)
            xg[q, 0, :, lanes(tile)] = scaled[0]
            xg[q, 1, :, lanes(tile)] = scaled[1]
            value = nn3((left[0], left[1]), scaled)
            if q == 2:
                dec[block, :, lane] = factor[length - 1 : length, :]
            if q in (0, 3):
                value = value * dec[block, :, lane]
            v[batch, block, :, int(q in (0, 3)), :, lane] = value.reshape(CHIPS, 8, TILE)

    def to_partner(batch):
        copies = [remote(v.at[batch, other], pv.at[batch], pair_send.at[batch], pair_recv.at[batch], partner)]
        if batch == 0:
            copies.append(remote(dec.at[other], pdec, pair_send.at[2], pair_recv.at[2], partner))
        for copy in copies:
            copy.start()
        return copies

    def gather(batch):
        own_decay = dec[core]
        mate_decay = pdec[...]
        if batch == 0:
            dc[0] = own_decay * mate_decay
        weights = (
            (first + second * mate_decay, first * own_decay + second),
            (first * mate_decay + second, first + second * own_decay),
        )

        def join(index):
            for flow in range(2):
                a, b = weights[flow]
                vc[batch, index, flow] = a * v[batch, core, index, flow] + b * pv[batch, index, flow]

        copies = []
        for offset in range(CHIPS - 1):
            there = peer(offset)
            join(there)
            device = (2 * there + core, zed)
            n = batch * CHIPS + offset
            copies.append(remote(vc.at[batch, there], r1.at[batch, chip], out_send.at[n], out_recv.at[n], device))
            copies[-1].start()
            if batch == 0:
                copies.append(remote(dc.at[0], dr.at[chip], dec_send.at[offset], dec_recv.at[offset], device))
                copies[-1].start()
        join(chip)
        r1[batch, chip] = vc[batch, chip]
        if batch == 0:
            dr[chip] = dc[0]
        return copies

    def scan_chips(batch, arrived):
        for copy in arrived:
            copy.wait()
        state = jnp.zeros((8, 2 * TILE), F32)
        for index in range(CHIPS):
            r2[batch, index, 1] = state
            state = r1[batch, index, 1] + dr[index] * state
        state = jnp.zeros((8, 2 * TILE), F32)
        for index in reversed(range(CHIPS)):
            r2[batch, index, 0] = state
            state = r1[batch, index, 0] + dr[index] * state
        copies = []
        for offset in range(CHIPS - 1):
            there = peer(offset)
            n = batch * CHIPS + offset
            copies.append(remote(r2.at[batch, there], r3.at[batch, chip], back_send.at[n], back_recv.at[n], (2 * there + core, zed)))
            copies[-1].start()
        r3[batch, chip] = r2[batch, chip]
        return copies

    def arrive(batch, returned):
        for copy in returned:
            copy.wait()
        own_decay = dec[core]
        mate_decay = pdec[...]

        def one(index, carry):
            for flow in range(2):
                mine, mate = (second, first) if flow == 0 else (first, second)
                value = r3[batch, index, flow]
                ein[batch, core, index, flow] = (mine + mate * mate_decay) * value + mate * pv[batch, index, flow]
                eout[batch, index, flow] = (mate + mine * own_decay) * value + mine * v[batch, core, index, flow]
            return carry

        lax.fori_loop(0, CHIPS, one, 0)
        give = remote(eout.at[batch], ein.at[batch, core], give_send.at[batch], give_recv.at[batch], partner)
        give.start()
        return give

    def project(batch, block, offset):
        tile = 2 * block + offset // TILE
        lane = slice(offset, offset + TILE)
        whole = dec[block, :, lane]
        early, late = [ein[batch, block, :, flow, :, lane].reshape(STATE, TILE) for flow in range(2)]
        if batch == 0:
            scaled = ((2, split2(whole * early)), (3, split2(late)))
        else:
            scaled = ((0, split2(late)), (1, split2(whole * early)))
            adjoint_early, adjoint_late = [ein[0, block, :, flow, :, lane].reshape(STATE, TILE) for flow in range(2)]
            local_early, local_late = [v[1, block, :, flow, :, lane].reshape(STATE, TILE) for flow in range(2)]
            edge[0:1, lanes(tile)] = jnp.sum(adjoint_early * (local_late + whole * late), axis=0, keepdims=True)
            edge[1:2, lanes(tile)] = jnp.sum(adjoint_late * (local_early + whole * early), axis=0, keepdims=True)
        total = None
        for m, value in scaled:
            es[m, 0, :, lanes(tile)] = value[0]
            es[m, 1, :, lanes(tile)] = value[1]
            term = nt3(pair(xg.at[(m + 2) % 4], slice(None), lanes(tile)), value)
            total = term if total is None else total + term
        for r in range(2):
            acc[batch, r] += total[r * half : (r + 1) * half]

    def exchange(batch, step_index, src, dst, targets):
        copies = []
        for r in range(2):
            n = 4 * batch + 2 * step_index + r
            copies.append(remote(src.at[batch, r], dst.at[batch, r], z_send.at[n], z_recv.at[n], (seq, targets[r])))
            copies[-1].start()
        return copies

    def exchange_again(batch, copies):
        for copy in copies:
            copy.wait()
        acc2[batch] = acc[batch] + z1[batch]
        return exchange(batch, 1, acc2, z2, (z_odd, z_even))

    def exchange_end(batch, copies, out):
        for copy in copies:
            copy.wait()
        for r in range(2):
            out[r * half : (r + 1) * half] = acc2[batch, r] + z2[batch, r]

    def add_heads(tile, terms):
        r = iota((TILE, STATE), 0)
        col = iota((TILE, STATE), 1)
        total = red[...]
        for m, term in terms:
            hot = (col == 16 * m + tile * 4 + r // HEAD_DIM).astype(F32).astype(BF16)
            a, b = split2(term)
            total = total + (nn(a, hot) + nn(b, hot))
        red[...] = total

    def finish_inputs(tile, carry):
        lane = lanes(tile)
        full = slice(None)
        b_pair = (bs[0], bs[1])
        in_f = fac[0, :, lane] * (inner[2, :, lane] + nn3(b_pair, pair(es.at[2], full, lane)))
        in_b = fac[1, :, lane] * (inner[3, :, lane] + nn3(b_pair, pair(es.at[3], full, lane)))
        gx_ref[:, lane] = in_f + in_b
        x = x_ref[:, lane]
        add_heads(tile, ((0, x * in_f), (1, x * in_b)))
        return carry

    def finish_outputs(tile, carry):
        lane = lanes(tile)
        full = slice(None)
        c_pair = (cs[0], cs[1])
        out_f = fac[2, :, lane] * (inner[0, :, lane] + nn3(c_pair, pair(es.at[0], full, lane)))
        out_b = fac[3, :, lane] * (inner[1, :, lane] + nn3(c_pair, pair(es.at[1], full, lane)))
        g = g_ref[:, lane]
        add_heads(tile, ((2, g * out_f), (3, g * out_b)))
        return carry

    def masked(m, source, tile, slot):
        lower = m in (0, 3)
        for r in range(2):
            row = slice(r * half, (r + 1) * half)
            depth = slice(0, (r + 1) * half) if lower else slice(r * half, length)
            left = (gm[m, 0, row, depth], gm[m, 1, row, depth])
            right = (xg[source, 0, depth, lanes(tile)], xg[source, 1, depth, lanes(tile)])
            inner[slot, row, lanes(tile)] = nn3(left, right)

    def input_side(tile, carry):
        masked(2, 2, tile, 2)
        masked(3, 3, tile, 3)
        return carry

    def output_side(tile, carry):
        masked(0, 0, tile, 0)
        masked(1, 1, tile, 1)
        return carry

    def square_side(tile, carry):
        low = iota((half, half), 0) >= iota((half, half), 1)
        high = iota((half, half), 0) <= iota((half, half), 1)
        upper = slice(0, half)
        under = slice(half, length)

        def block(a, row, b, col):
            return nt3(pair(xg.at[a], row, lanes(tile)), pair(xg.at[b], col, lanes(tile)))

        for part in (upper, under):
            amat[part, part] += jnp.where(low, block(2, part, 0, part), 0.0) + jnp.where(high, block(3, part, 1, part), 0.0)
        amat[under, upper] += block(2, under, 0, upper)
        amat[upper, under] += block(3, upper, 1, under)
        return carry

    loads[2].wait()
    turn(c_ref, cs, ct)
    loads[3].wait()
    for j in range(2):
        summarise(0, 2 * other + j, other, j * TILE)
    pl.semaphore_wait(barrier, CHIPS + 2)
    copies = to_partner(0)
    for j in range(2):
        summarise(0, 2 * core + j, core, j * TILE)
    for copy in copies:
        copy.wait()
    out_0 = gather(0)

    loads[4].wait()
    turn(b_ref, bs, bt)
    loads[5].wait()
    for j in range(2):
        summarise(1, 2 * other + j, other, j * TILE)
    copies = to_partner(1)
    for j in range(2):
        summarise(1, 2 * core + j, core, j * TILE)
    for copy in copies:
        copy.wait()
    out_1 = gather(1)

    for r in range(2):
        row = slice(r * half, (r + 1) * half)
        forward = nt3((cs[0, row], cs[1, row]), (bs[0], bs[1]))
        backward = nt3((bs[0, row], bs[1, row]), (cs[0], cs[1]))
        i = iota((half, length), 0) + r * half
        j = iota((half, length), 1)
        for m, (value, keep) in enumerate(((forward, i >= j), (forward, i <= j), (backward, i <= j), (backward, i >= j))):
            gm[m, 0, row], gm[m, 1, row] = split2(jnp.where(keep, value, 0.0))
    lax.fori_loop(0, 4, input_side, 0)

    back_0 = scan_chips(0, out_0)
    amat[...] = jnp.zeros_like(amat)
    red[...] = jnp.zeros_like(red)
    edge[...] = jnp.zeros_like(edge)
    lax.fori_loop(0, 4, square_side, 0)

    back_1 = scan_chips(1, out_1)
    whole_a = amat[...]
    from_b = nn3(split2(whole_a), (bs[0], bs[1]))
    from_c = nn3(split2(jnp.transpose(whole_a)), (cs[0], cs[1]))
    for r in range(2):
        acc[0, r] = from_c[r * half : (r + 1) * half]
        acc[1, r] = from_b[r * half : (r + 1) * half]
    lax.fori_loop(0, 4, output_side, 0)

    give = arrive(0, back_0)
    for j in range(2):
        project(0, core, j * TILE)
    give.wait()
    for j in range(2):
        project(0, other, j * TILE)
    zed_0 = exchange(0, 0, acc, z1, (z_even, z_odd))
    lax.fori_loop(0, 4, finish_inputs, 0)
    store = pltpu.make_async_copy(gx_ref, gx_hbm, store_sem.at[0])
    store.start()
    zed_0 = exchange_again(0, zed_0)

    give = arrive(1, back_1)
    for j in range(2):
        project(1, core, j * TILE)
    give.wait()
    for j in range(2):
        project(1, other, j * TILE)
    zed_1 = exchange(1, 0, acc, z1, (z_even, z_odd))
    exchange_end(0, zed_0, gb_ref)
    lax.fori_loop(0, 3, finish_outputs, 0)
    zed_1 = exchange_again(1, zed_1)
    lax.fori_loop(3, 4, finish_outputs, 0)

    sums = jnp.transpose(red[...])
    in_f, in_b, out_f, out_b = [sums[16 * m : 16 * m + heads] for m in range(4)]
    hot = (iota((4 * TILE, STATE), 1) == iota((4 * TILE, STATE), 0) // HEAD_DIM).astype(F32).astype(BF16)
    edges = [nn(p, hot) for p in split3(edge[...])]
    edges = jnp.transpose(edges[0] + (edges[1] + edges[2]))
    after = (rows >= cols).astype(F32).astype(BF16)

    def running(value, matrix):
        out = nn(jnp.concatenate(split3(value), axis=0), matrix)
        return out[:heads] + (out[heads : 2 * heads] + out[2 * heads :])

    log_grad = running(out_f - in_f, after) + edges[:heads, 0:1]
    log_grad = log_grad + running(out_b - in_b, upto) + edges[:heads, 1:2]
    graw_ref[...] = ((in_f + in_b) / step - rate * log_grad) * jax.nn.sigmoid(raw)

    exchange_end(1, zed_1, gc_ref)
    store.wait()


def hand_over(*refs):
    sources, targets, buffers, load_sem, store_sem = refs[:4], refs[4:8], refs[8:12], refs[12], refs[13]
    pieces = []
    for n in range(4):
        parts = 4 if n == 0 else 1
        rows = sources[n].shape[0] // parts
        pieces += [(n, pl.ds(p * rows, rows)) for p in range(parts)]
    loads = []
    for i, (n, row) in enumerate(pieces):
        loads.append(pltpu.make_async_copy(sources[n].at[row], buffers[n].at[row], load_sem.at[i]))
        loads[-1].start()
    stores = []
    for i, (n, row) in enumerate(pieces):
        loads[i].wait()
        stores.append(pltpu.make_async_copy(buffers[n].at[row], targets[n].at[row], store_sem.at[i]))
        stores[-1].start()
    for copy in stores:
        copy.wait()


def on_device(inputs, step_raw, decay_rate, b_proj, c_proj, grad_out):
    length, width = inputs.shape
    heads = step_raw.shape[0]
    vmem = pl.BlockSpec(memory_space=pltpu.VMEM)
    anywhere = pl.BlockSpec(memory_space=pl.ANY)
    block = (CHIPS, 2, 8, width // 2)
    square = (length, length)
    half = length // 2
    dma = pltpu.SemaphoreType.DMA
    scratch = [
        pltpu.VMEM((length, width), F32),
        pltpu.VMEM((length, width), F32),
        pltpu.VMEM((heads, length), F32),
        pltpu.VMEM((1, heads), F32),
        pltpu.VMEM((length, STATE), F32),
        pltpu.VMEM((length, STATE), F32),
        pltpu.VMEM((length, width), F32),
        pltpu.VMEM((length, 256), BF16),
        pltpu.VMEM((4, length, width), F32),
        pltpu.VMEM((4, 2, length, width), BF16),
        pltpu.VMEM((2, STATE, length), BF16),
        pltpu.VMEM((2, STATE, length), BF16),
        pltpu.VMEM((2, length, STATE), BF16),
        pltpu.VMEM((2, length, STATE), BF16),
        pltpu.VMEM((4, 2) + square, BF16),
        pltpu.VMEM(square, F32),
        pltpu.VMEM((4, length, width), F32),
        pltpu.VMEM((2, 2) + block, F32),
        pltpu.VMEM((2, 1, width // 2), F32),
        pltpu.VMEM((2,) + block, F32),
        pltpu.VMEM((1, width // 2), F32),
        pltpu.VMEM((2,) + block, F32),
        pltpu.VMEM((1, 1, width // 2), F32),
        pltpu.VMEM((2,) + block, F32),
        pltpu.VMEM((CHIPS, 1, width // 2), F32),
        pltpu.VMEM((2,) + block, F32),
        pltpu.VMEM((2,) + block, F32),
        pltpu.VMEM((2, 2) + block, F32),
        pltpu.VMEM((2,) + block, F32),
        pltpu.VMEM((4, 2, STATE, width), BF16),
        pltpu.VMEM((8, width), F32),
        pltpu.VMEM((2, 2, half, STATE), F32),
        pltpu.VMEM((2, 2, half, STATE), F32),
        pltpu.VMEM((2, 2, half, STATE), F32),
        pltpu.VMEM((2, 2, half, STATE), F32),
        pltpu.VMEM((length, STATE), F32),
        dma((6,)),
        dma((1,)),
        dma((3,)),
        dma((3,)),
        dma((2 * CHIPS,)),
        dma((2 * CHIPS,)),
        dma((CHIPS,)),
        dma((CHIPS,)),
        dma((2 * CHIPS,)),
        dma((2 * CHIPS,)),
        dma((2,)),
        dma((2,)),
        dma((8,)),
        dma((8,)),
    ]
    shapes = ((length, width), (heads, length), (length, STATE), (length, STATE))
    out_shape = tuple(jax.ShapeDtypeStruct(shape, F32) for shape in shapes)
    results = pl.pallas_call(
        kernel,
        out_shape=out_shape,
        in_specs=[anywhere] * 6,
        out_specs=(anywhere, vmem, vmem, vmem),
        scratch_shapes=scratch,
        compiler_params=pltpu.CompilerParams(
            collective_id=0, has_side_effects=True, vmem_limit_bytes=67043328
        ),
        name="scan_backward",
    )(inputs, grad_out, step_raw, decay_rate.reshape(1, heads), b_proj, c_proj)
    return pl.pallas_call(
        hand_over,
        out_shape=out_shape,
        in_specs=[anywhere] * 4,
        out_specs=(anywhere,) * 4,
        scratch_shapes=[pltpu.VMEM(shape, F32) for shape in shapes] + [dma((7,)), dma((7,))],
        name="hand_over",
    )(*results)


def solution(mesh):
    return jax.shard_map(
        on_device,
        mesh=mesh,
        in_specs=(
            P("seq", "head"),
            P("head", "seq"),
            P("head"),
            P("seq", None),
            P("seq", None),
            P("seq", "head"),
        ),
        out_specs=(P("seq", "head"), P("head", "seq"), P("seq", None), P("seq", None)),
        check_vma=False,
    )
```

time: 74.8 us -> 63.5 us (0.85)
  the two profiles are of different devices: /device:TPU:1 before, /device:TPU:6 now
where the time goes in v1:
time: 63.5 us; the launch traced here: 63.4 us
  Pallas kernels  62.6 us (99%)
  between operations  0.8 us (1%)
    pallas_call x1, Pallas kernels, on_device(): pl.pallas_call(kernel, out_shape=out_shape, in_specs=[anywhere] * 6, out_...  59.9 us
    pallas_call x1, Pallas kernels, on_device(): pl.pallas_call(hand_over, out_shape=out_shape, in_specs=[anywhere] * 4, o...  2.65 us

profile of v1, /device:TPU:6, one launch (start us, length us, event | category | flops | bytes accessed | tf_op | source)
XLA Modules:
  0.0 63.4 jit_solution(13723802470232684216)
XLA Ops:
  0.6 59.9 %scan_backward.1 = (f32[512,1024]{1,0:T(8,128)}, f32[16,512]{1,0:T(8,128)}, f32[512,128]{1,0:T(8,128)}, f32[512,128]{1,0:T(8,128)}) custom-call(f32[512,1024]{1,0:T(8,128)} %x_hbm.1, f32[512,1024]{1,0:T(8,128)} %g_hbm.1, f32[16,512]{1,0:T(8,128)} %raw_hbm.1, f32[1,16]{1,0:T(1,128)} %bitcast.1, f32[512,128]{1,0:T(8,128)} %b_hbm.1, f32[512,128]{1,0:T(8,128)} %c_hbm.1), custom_call_target="tpu_custom_call" | custom-call | tf_op jit(solution)/shard_map/scan_backward/pallas_call | solution.py:514
  60.6 2.7 %hand_over.1 = (f32[512,1024]{1,0:T(8,128)}, f32[16,512]{1,0:T(8,128)}, f32[512,128]{1,0:T(8,128)}, f32[512,128]{1,0:T(8,128)}) custom-call(f32[512,1024]{1,0:T(8,128)} %get-tuple-element.8.refs_0_, f32[16,512]{1,0:T(8,128)} %get-tuple-element.9.refs_1_, f32[512,128]{1,0:T(8,128)} %get-tuple-element.10.refs_2_, f32[512,128]{1,0:T(8,128)} %get-tuple-element.11.refs_3_), custom_call_target="tpu_custom_call" | custom-call | tf_op jit(solution)/shard_map/hand_over/pallas_call | solution.py:525

commit v2 on v1

--- a/solution.py
+++ b/solution.py
@@ -46,6 +46,7 @@
     return lax.broadcasted_iota(jnp.int32, shape, axis)
 
 
+SOON = 15
 OFFSETS = sorted(
     ((dx, dy) for dx in range(4) for dy in range(4) if dx or dy),
     key=lambda o: -(min(o[0], 4 - o[0]) + min(o[1], 4 - o[1])),
@@ -75,6 +76,7 @@
     length = x_ref.shape[0]
     heads = raw_ref.shape[0]
     half = length // 2
+    quarter = half // 2
     first = (core == 0).astype(F32)
     second = 1.0 - first
 
@@ -122,8 +124,14 @@
 
     def turn(src, flat, turned):
         full = src[...]
-        flat[0], flat[1] = split2(full)
+        high, low = split2(full)
+        flat[:, :STATE] = high
+        flat[:, STATE : 2 * STATE] = high
+        flat[:, 2 * STATE :] = low
         turned[0], turned[1] = split2(jnp.transpose(full))
+
+    def halves(flat, row=slice(None)):
+        return flat[row, :STATE], flat[row, 2 * STATE :]
 
     def pair(ref, *index):
         return ref[(0,) + index], ref[(1,) + index]
@@ -157,7 +165,7 @@
             copy.start()
         return copies
 
-    def gather(batch):
+    def gather(batch, offsets=range(CHIPS - 1)):
         own_decay = dec[core]
         mate_decay = pdec[...]
         if batch == 0:
@@ -173,7 +181,7 @@
                 vc[batch, index, flow] = a * v[batch, core, index, flow] + b * pv[batch, index, flow]
 
         copies = []
-        for offset in range(CHIPS - 1):
+        for offset in offsets:
             there = peer(offset)
             join(there)
             device = (2 * there + core, zed)
@@ -183,15 +191,16 @@
             if batch == 0:
                 copies.append(remote(dc.at[0], dr.at[chip], dec_send.at[offset], dec_recv.at[offset], device))
                 copies[-1].start()
-        join(chip)
-        r1[batch, chip] = vc[batch, chip]
+        if CHIPS - 2 in offsets:
+            join(chip)
+            r1[batch, chip] = vc[batch, chip]
         if batch == 0:
             dr[chip] = dc[0]
         return copies
 
     def scan_chips(batch, arrived):
         for copy in arrived:
-            copy.wait()
+            copy.wait_recv()
         state = jnp.zeros((8, 2 * TILE), F32)
         for index in range(CHIPS):
             r2[batch, index, 1] = state
@@ -210,23 +219,24 @@
         return copies
 
     def arrive(batch, returned):
-        for copy in returned:
-            copy.wait()
         own_decay = dec[core]
         mate_decay = pdec[...]
-
-        def one(index, carry):
+        gives = []
+        for offset in range(-1, CHIPS - 1):
+            index = chip
+            if offset >= 0:
+                dx, dy = OFFSETS[offset]
+                index = ((chip_x + 4 - dx) % 4) * 4 + (chip_y + 4 - dy) % 4
+                returned[offset].wait_recv()
             for flow in range(2):
                 mine, mate = (second, first) if flow == 0 else (first, second)
                 value = r3[batch, index, flow]
                 ein[batch, core, index, flow] = (mine + mate * mate_decay) * value + mate * pv[batch, index, flow]
                 eout[batch, index, flow] = (mate + mine * own_decay) * value + mine * v[batch, core, index, flow]
-            return carry
-
-        lax.fori_loop(0, CHIPS, one, 0)
-        give = remote(eout.at[batch], ein.at[batch, core], give_send.at[batch], give_recv.at[batch], partner)
-        give.start()
-        return give
+            n = batch * CHIPS + offset + 1
+            gives.append(remote(eout.at[batch, index], ein.at[batch, core, index], give_send.at[n], give_recv.at[n], partner))
+            gives[-1].start()
+        return gives
 
     def project(batch, block, offset):
         tile = 2 * block + offset // TILE
@@ -243,32 +253,39 @@
             edge[1:2, lanes(tile)] = jnp.sum(adjoint_late * (local_early + whole * early), axis=0, keepdims=True)
         total = None
         for m, value in scaled:
-            es[m, 0, :, lanes(tile)] = value[0]
-            es[m, 1, :, lanes(tile)] = value[1]
-            term = nt3(pair(xg.at[(m + 2) % 4], slice(None), lanes(tile)), value)
+            es[m, :STATE, lanes(tile)] = value[0]
+            es[m, STATE : 2 * STATE, lanes(tile)] = value[1]
+            es[m, 2 * STATE :, lanes(tile)] = value[0]
+            high, low = pair(xg.at[(m + 2) % 4], slice(None), lanes(tile))
+            wide = nt(high, jnp.concatenate(value, axis=0))
+            term = wide[:, :STATE] + (wide[:, STATE:] + nt(low, value[0]))
             total = term if total is None else total + term
-        for r in range(2):
-            acc[batch, r] += total[r * half : (r + 1) * half]
-
-    def exchange(batch, step_index, src, dst, targets):
-        copies = []
-        for r in range(2):
-            n = 4 * batch + 2 * step_index + r
-            copies.append(remote(src.at[batch, r], dst.at[batch, r], z_send.at[n], z_recv.at[n], (seq, targets[r])))
-            copies[-1].start()
-        return copies
+        acc[batch] += total.reshape(2, 2, quarter, STATE)
+
+    def exchange_part(batch, step_index, src, dst, part, r, targets):
+        n = 8 * batch + 4 * step_index + 2 * part + r
+        copy = remote(src.at[batch, r, part], dst.at[batch, r, part], z_send.at[n], z_recv.at[n], (seq, targets[r]))
+        copy.start()
+        return copy
+
+    def exchange(batch):
+        return [exchange_part(batch, 0, acc, z1, part, r, (z_even, z_odd)) for part in range(2) for r in range(2)]
 
     def exchange_again(batch, copies):
-        for copy in copies:
-            copy.wait()
-        acc2[batch] = acc[batch] + z1[batch]
-        return exchange(batch, 1, acc2, z2, (z_odd, z_even))
+        onward = []
+        for part in range(2):
+            for r in range(2):
+                copies[2 * part + r].wait()
+                acc2[batch, r, part] = acc[batch, r, part] + z1[batch, r, part]
+                onward.append(exchange_part(batch, 1, acc2, z2, part, r, (z_odd, z_even)))
+        return onward
 
     def exchange_end(batch, copies, out):
-        for copy in copies:
-            copy.wait()
-        for r in range(2):
-            out[r * half : (r + 1) * half] = acc2[batch, r] + z2[batch, r]
+        for part in range(2):
+            for r in range(2):
+                copies[2 * part + r].wait()
+                start = r * half + part * quarter
+                out[start : start + quarter] = acc2[batch, r, part] + z2[batch, r, part]
 
     def add_heads(tile, terms):
         r = iota((TILE, STATE), 0)
@@ -282,10 +299,8 @@
 
     def finish_inputs(tile, carry):
         lane = lanes(tile)
-        full = slice(None)
-        b_pair = (bs[0], bs[1])
-        in_f = fac[0, :, lane] * (inner[2, :, lane] + nn3(b_pair, pair(es.at[2], full, lane)))
-        in_b = fac[1, :, lane] * (inner[3, :, lane] + nn3(b_pair, pair(es.at[3], full, lane)))
+        in_f = fac[0, :, lane] * (inner[2, :, lane] + nn(bs[...], es[2, :, lane]))
+        in_b = fac[1, :, lane] * (inner[3, :, lane] + nn(bs[...], es[3, :, lane]))
         gx_ref[:, lane] = in_f + in_b
         x = x_ref[:, lane]
         add_heads(tile, ((0, x * in_f), (1, x * in_b)))
@@ -293,10 +308,8 @@
 
     def finish_outputs(tile, carry):
         lane = lanes(tile)
-        full = slice(None)
-        c_pair = (cs[0], cs[1])
-        out_f = fac[2, :, lane] * (inner[0, :, lane] + nn3(c_pair, pair(es.at[0], full, lane)))
-        out_b = fac[3, :, lane] * (inner[1, :, lane] + nn3(c_pair, pair(es.at[1], full, lane)))
+        out_f = fac[2, :, lane] * (inner[0, :, lane] + nn(cs[...], es[0, :, lane]))
+        out_b = fac[3, :, lane] * (inner[1, :, lane] + nn(cs[...], es[1, :, lane]))
         g = g_ref[:, lane]
         add_heads(tile, ((2, g * out_f), (3, g * out_b)))
         return carry
@@ -340,74 +353,84 @@
     loads[3].wait()
     for j in range(2):
         summarise(0, 2 * other + j, other, j * TILE)
-    pl.semaphore_wait(barrier, CHIPS + 2)
-    copies = to_partner(0)
     for j in range(2):
         summarise(0, 2 * core + j, core, j * TILE)
-    for copy in copies:
-        copy.wait()
-    out_0 = gather(0)
-
     loads[4].wait()
     turn(b_ref, bs, bt)
     loads[5].wait()
     for j in range(2):
         summarise(1, 2 * other + j, other, j * TILE)
-    copies = to_partner(1)
     for j in range(2):
         summarise(1, 2 * core + j, core, j * TILE)
-    for copy in copies:
+
+    pl.semaphore_wait(barrier, CHIPS + 2)
+    pair_0 = to_partner(0)
+    pair_1 = to_partner(1)
+    amat[...] = jnp.zeros_like(amat)
+    red[...] = jnp.zeros_like(red)
+    edge[...] = jnp.zeros_like(edge)
+    for copy in pair_0:
+        copy.wait()
+    out_0 = gather(0)
+    for copy in pair_1:
         copy.wait()
     out_1 = gather(1)
 
     for r in range(2):
         row = slice(r * half, (r + 1) * half)
-        forward = nt3((cs[0, row], cs[1, row]), (bs[0], bs[1]))
-        backward = nt3((bs[0, row], bs[1, row]), (cs[0], cs[1]))
+        forward = nt3(halves(cs, row), halves(bs))
+        backward = nt3(halves(bs, row), halves(cs))
         i = iota((half, length), 0) + r * half
         j = iota((half, length), 1)
         for m, (value, keep) in enumerate(((forward, i >= j), (forward, i <= j), (backward, i <= j), (backward, i >= j))):
             gm[m, 0, row], gm[m, 1, row] = split2(jnp.where(keep, value, 0.0))
     lax.fori_loop(0, 4, input_side, 0)
 
+    lax.fori_loop(0, 4, square_side, 0)
     back_0 = scan_chips(0, out_0)
-    amat[...] = jnp.zeros_like(amat)
-    red[...] = jnp.zeros_like(red)
-    edge[...] = jnp.zeros_like(edge)
-    lax.fori_loop(0, 4, square_side, 0)
-
+    for copy in out_0:
+        copy.wait_send()
+
+    whole_a = amat[...]
+    from_b = nn3(split2(whole_a), halves(bs))
+    from_c = nn3(split2(jnp.transpose(whole_a)), halves(cs))
+    acc[0] = from_c.reshape(2, 2, quarter, STATE)
+    acc[1] = from_b.reshape(2, 2, quarter, STATE)
+    lax.fori_loop(0, 4, output_side, 0)
+
+    for copy in back_0:
+        copy.wait_send()
+    for copy in out_1:
+        copy.wait_send()
     back_1 = scan_chips(1, out_1)
-    whole_a = amat[...]
-    from_b = nn3(split2(whole_a), (bs[0], bs[1]))
-    from_c = nn3(split2(jnp.transpose(whole_a)), (cs[0], cs[1]))
-    for r in range(2):
-        acc[0, r] = from_c[r * half : (r + 1) * half]
-        acc[1, r] = from_b[r * half : (r + 1) * half]
-    lax.fori_loop(0, 4, output_side, 0)
-
-    give = arrive(0, back_0)
+    gives = arrive(0, back_0)
     for j in range(2):
         project(0, core, j * TILE)
-    give.wait()
+    for give in gives:
+        give.wait()
     for j in range(2):
         project(0, other, j * TILE)
-    zed_0 = exchange(0, 0, acc, z1, (z_even, z_odd))
-    lax.fori_loop(0, 4, finish_inputs, 0)
+    zed_0 = exchange(0)
+    lax.fori_loop(0, 2, finish_inputs, 0)
+    zed_0 = exchange_again(0, zed_0)
+
+    for copy in back_1:
+        copy.wait_send()
+    gives = arrive(1, back_1)
+    for j in range(2):
+        project(1, core, j * TILE)
+    for give in gives:
+        give.wait()
+    for j in range(2):
+        project(1, other, j * TILE)
+    zed_1 = exchange(1)
+    lax.fori_loop(2, 4, finish_inputs, 0)
     store = pltpu.make_async_copy(gx_ref, gx_hbm, store_sem.at[0])
     store.start()
-    zed_0 = exchange_again(0, zed_0)
-
-    give = arrive(1, back_1)
-    for j in range(2):
-        project(1, core, j * TILE)
-    give.wait()
-    for j in range(2):
-        project(1, other, j * TILE)
-    zed_1 = exchange(1, 0, acc, z1, (z_even, z_odd))
     exchange_end(0, zed_0, gb_ref)
-    lax.fori_loop(0, 3, finish_outputs, 0)
+    lax.fori_loop(0, 2, finish_outputs, 0)
     zed_1 = exchange_again(1, zed_1)
-    lax.fori_loop(3, 4, finish_outputs, 0)
+    lax.fori_loop(2, 4, finish_outputs, 0)
 
     sums = jnp.transpose(red[...])
     in_f, in_b, out_f, out_b = [sums[16 * m : 16 * m + heads] for m in range(4)]
@@ -432,7 +455,7 @@
     sources, targets, buffers, load_sem, store_sem = refs[:4], refs[4:8], refs[8:12], refs[12], refs[13]
     pieces = []
     for n in range(4):
-        parts = 4 if n == 0 else 1
+        parts = 8 if n == 0 else 1
         rows = sources[n].shape[0] // parts
         pieces += [(n, pl.ds(p * rows, rows)) for p in range(parts)]
     loads = []
@@ -470,8 +493,8 @@
         pltpu.VMEM((4, 2, length, width), BF16),
         pltpu.VMEM((2, STATE, length), BF16),
         pltpu.VMEM((2, STATE, length), BF16),
-        pltpu.VMEM((2, length, STATE), BF16),
-        pltpu.VMEM((2, length, STATE), BF16),
+        pltpu.VMEM((length, 3 * STATE), BF16),
+        pltpu.VMEM((length, 3 * STATE), BF16),
         pltpu.VMEM((4, 2) + square, BF16),
         pltpu.VMEM(square, F32),
         pltpu.VMEM((4, length, width), F32),
@@ -487,12 +510,12 @@
         pltpu.VMEM((2,) + block, F32),
         pltpu.VMEM((2, 2) + block, F32),
         pltpu.VMEM((2,) + block, F32),
-        pltpu.VMEM((4, 2, STATE, width), BF16),
+        pltpu.VMEM((4, 3 * STATE, width), BF16),
         pltpu.VMEM((8, width), F32),
-        pltpu.VMEM((2, 2, half, STATE), F32),
-        pltpu.VMEM((2, 2, half, STATE), F32),
-        pltpu.VMEM((2, 2, half, STATE), F32),
-        pltpu.VMEM((2, 2, half, STATE), F32),
+        pltpu.VMEM((2, 2, 2, half // 2, STATE), F32),
+        pltpu.VMEM((2, 2, 2, half // 2, STATE), F32),
+        pltpu.VMEM((2, 2, 2, half // 2, STATE), F32),
+        pltpu.VMEM((2, 2, 2, half // 2, STATE), F32),
         pltpu.VMEM((length, STATE), F32),
         dma((6,)),
         dma((1,)),
@@ -504,10 +527,10 @@
         dma((CHIPS,)),
         dma((2 * CHIPS,)),
         dma((2 * CHIPS,)),
-        dma((2,)),
-        dma((2,)),
-        dma((8,)),
-        dma((8,)),
+        dma((2 * CHIPS,)),
+        dma((2 * CHIPS,)),
+        dma((16,)),
+        dma((16,)),
     ]
     shapes = ((length, width), (heads, length), (length, STATE), (length, STATE))
     out_shape = tuple(jax.ShapeDtypeStruct(shape, F32) for shape in shapes)
@@ -527,7 +550,7 @@
         out_shape=out_shape,
         in_specs=[anywhere] * 4,
         out_specs=(anywhere,) * 4,
-        scratch_shapes=[pltpu.VMEM(shape, F32) for shape in shapes] + [dma((7,)), dma((7,))],
+        scratch_shapes=[pltpu.VMEM(shape, F32) for shape in shapes] + [dma((11,)), dma((11,))],
         name="hand_over",
     )(*results)
 

time: 63.5 us -> 60 us (0.945)
  the two profiles are of different devices: /device:TPU:6 before, /device:TPU:1 now
where the time goes in v2:
time: 60 us; the launch traced here: 59.8 us
  Pallas kernels  59 us (98%)
  between operations  0.8 us (1%)
    pallas_call x1, Pallas kernels, on_device(): pl.pallas_call(kernel, out_shape=out_shape, in_specs=[anywhere] * 6, out_...  56.4 us
    pallas_call x1, Pallas kernels, on_device(): pl.pallas_call(hand_over, out_shape=out_shape, in_specs=[anywhere] * 4, o...  2.63 us

profile of v2, /device:TPU:1, one launch (start us, length us, event | category | flops | bytes accessed | tf_op | source)
XLA Modules:
  0.0 59.8 jit_solution(8508859174899033120)
XLA Ops:
  0.6 56.4 %scan_backward.1 = (f32[512,1024]{1,0:T(8,128)}, f32[16,512]{1,0:T(8,128)}, f32[512,128]{1,0:T(8,128)}, f32[512,128]{1,0:T(8,128)}) custom-call(f32[512,1024]{1,0:T(8,128)} %x_hbm.1, f32[512,1024]{1,0:T(8,128)} %g_hbm.1, f32[16,512]{1,0:T(8,128)} %raw_hbm.1, f32[1,16]{1,0:T(1,128)} %bitcast.1, f32[512,128]{1,0:T(8,128)} %b_hbm.1, f32[512,128]{1,0:T(8,128)} %c_hbm.1), custom_call_target="tpu_custom_call" | custom-call | tf_op jit(solution)/shard_map/scan_backward/pallas_call | solution.py:537
  57.0 2.6 %hand_over.1 = (f32[512,1024]{1,0:T(8,128)}, f32[16,512]{1,0:T(8,128)}, f32[512,128]{1,0:T(8,128)}, f32[512,128]{1,0:T(8,128)}) custom-call(f32[512,1024]{1,0:T(8,128)} %get-tuple-element.8.refs_0_, f32[16,512]{1,0:T(8,128)} %get-tuple-element.9.refs_1_, f32[512,128]{1,0:T(8,128)} %get-tuple-element.10.refs_2_, f32[512,128]{1,0:T(8,128)} %get-tuple-element.11.refs_3_), custom_call_target="tpu_custom_call" | custom-call | tf_op jit(solution)/shard_map/hand_over/pallas_call | solution.py:548

commit v3 on v2

--- a/solution.py
+++ b/solution.py
@@ -46,7 +46,6 @@
     return lax.broadcasted_iota(jnp.int32, shape, axis)
 
 
-SOON = 15
 OFFSETS = sorted(
     ((dx, dy) for dx in range(4) for dy in range(4) if dx or dy),
     key=lambda o: -(min(o[0], 4 - o[0]) + min(o[1], 4 - o[1])),
@@ -55,12 +54,12 @@
 
 def kernel(
     x_hbm, g_hbm, raw_hbm, rate_hbm, b_hbm, c_hbm,
-    gx_hbm, graw_ref, gb_ref, gc_ref,
-    x_ref, g_ref, raw_ref, rate_ref, b_ref, c_ref, gx_ref,
+    gx_ref, graw_ref, gb_ref, gc_ref,
+    x_ref, g_ref, raw_ref, rate_ref, b_ref, c_ref,
     ft, fac, xg, bt, ct, bs, cs, gm, amat, inner,
     v, dec, pv, pdec, vc, dc, r1, dr, r2, r3, ein, eout, es, edge,
     acc, z1, acc2, z2, red,
-    load_sem, store_sem, pair_send, pair_recv, out_send, out_recv, dec_send, dec_recv,
+    load_sem, pair_send, pair_recv, out_send, out_recv, dec_send, dec_recv,
     back_send, back_recv, give_send, give_recv, z_send, z_recv,
 ):
     seq = lax.axis_index("seq")
@@ -425,8 +424,6 @@
         project(1, other, j * TILE)
     zed_1 = exchange(1)
     lax.fori_loop(2, 4, finish_inputs, 0)
-    store = pltpu.make_async_copy(gx_ref, gx_hbm, store_sem.at[0])
-    store.start()
     exchange_end(0, zed_0, gb_ref)
     lax.fori_loop(0, 2, finish_outputs, 0)
     zed_1 = exchange_again(1, zed_1)
@@ -448,27 +445,6 @@
     graw_ref[...] = ((in_f + in_b) / step - rate * log_grad) * jax.nn.sigmoid(raw)
 
     exchange_end(1, zed_1, gc_ref)
-    store.wait()
-
-
-def hand_over(*refs):
-    sources, targets, buffers, load_sem, store_sem = refs[:4], refs[4:8], refs[8:12], refs[12], refs[13]
-    pieces = []
-    for n in range(4):
-        parts = 8 if n == 0 else 1
-        rows = sources[n].shape[0] // parts
-        pieces += [(n, pl.ds(p * rows, rows)) for p in range(parts)]
-    loads = []
-    for i, (n, row) in enumerate(pieces):
-        loads.append(pltpu.make_async_copy(sources[n].at[row], buffers[n].at[row], load_sem.at[i]))
-        loads[-1].start()
-    stores = []
-    for i, (n, row) in enumerate(pieces):
-        loads[i].wait()
-        stores.append(pltpu.make_async_copy(buffers[n].at[row], targets[n].at[row], store_sem.at[i]))
-        stores[-1].start()
-    for copy in stores:
-        copy.wait()
 
 
 def on_device(inputs, step_raw, decay_rate, b_proj, c_proj, grad_out):
@@ -487,7 +463,6 @@
         pltpu.VMEM((1, heads), F32),
         pltpu.VMEM((length, STATE), F32),
         pltpu.VMEM((length, STATE), F32),
-        pltpu.VMEM((length, width), F32),
         pltpu.VMEM((length, 256), BF16),
         pltpu.VMEM((4, length, width), F32),
         pltpu.VMEM((4, 2, length, width), BF16),
@@ -518,7 +493,6 @@
         pltpu.VMEM((2, 2, 2, half // 2, STATE), F32),
         pltpu.VMEM((length, STATE), F32),
         dma((6,)),
-        dma((1,)),
         dma((3,)),
         dma((3,)),
         dma((2 * CHIPS,)),
@@ -533,26 +507,18 @@
         dma((16,)),
     ]
     shapes = ((length, width), (heads, length), (length, STATE), (length, STATE))
-    out_shape = tuple(jax.ShapeDtypeStruct(shape, F32) for shape in shapes)
     results = pl.pallas_call(
         kernel,
-        out_shape=out_shape,
+        out_shape=tuple(pltpu.VMEM(shape, F32) for shape in shapes),
         in_specs=[anywhere] * 6,
-        out_specs=(anywhere, vmem, vmem, vmem),
+        out_specs=(vmem,) * 4,
         scratch_shapes=scratch,
         compiler_params=pltpu.CompilerParams(
-            collective_id=0, has_side_effects=True, vmem_limit_bytes=67043328
+            collective_id=0, has_side_effects=True, vmem_limit_bytes=60 * 2**20
         ),
         name="scan_backward",
     )(inputs, grad_out, step_raw, decay_rate.reshape(1, heads), b_proj, c_proj)
-    return pl.pallas_call(
-        hand_over,
-        out_shape=out_shape,
-        in_specs=[anywhere] * 4,
-        out_specs=(anywhere,) * 4,
-        scratch_shapes=[pltpu.VMEM(shape, F32) for shape in shapes] + [dma((11,)), dma((11,))],
-        name="hand_over",
-    )(*results)
+    return results
 
 
 def solution(mesh):

time: 60 us -> 59.6 us (level)
  Pallas kernels: 59 us -> 55.5 us
  local copies, waits for them, and re-layouts: 0 us -> 3.34 us
    pallas_call x2 -> x1, Pallas kernels: 59 us -> 55.5 us  [on_device(): pl.pallas_call(kernel, out_shape=tuple((pltpu.VMEM(shape, F32) for shape...]
    unnamed x0 -> x4, local copies, waits for them, and re-layouts: none -> 3.34 us
where the time goes in v3:
time: 59.6 us; the launch traced here: 59.5 us
  Pallas kernels  55.5 us (93%)
  local copies, waits for them, and re-layouts  3.34 us (6%)
  between operations  0.64 us (1%)
    pallas_call x1, Pallas kernels, on_device(): pl.pallas_call(kernel, out_shape=tuple((pltpu.VMEM(shape, F32) for shape...  55.5 us
    unnamed x4, local copies, waits for them, and re-layouts  3.34 us

profile of v3, /device:TPU:1, one launch (start us, length us, event | category | flops | bytes accessed | tf_op | source)
XLA Modules:
  0.0 59.5 jit_solution(12811748551628678769)
XLA Ops:
  0.6 55.5 %scan_backward.1 = (f32[512,1024]{1,0:T(8,128)S(1)}, f32[16,512]{1,0:T(8,128)S(1)}, f32[512,128]{1,0:T(8,128)S(1)}, f32[512,128]{1,0:T(8,128)S(1)}) custom-call(f32[512,1024]{1,0:T(8,128)} %x_hbm.1, f32[512,1024]{1,0:T(8,128)} %g_hbm.1, f32[16,512]{1,0:T(8,128)} %raw_hbm.1, f32[1,16]{1,0:T(1,128)} %bitcast.1, f32[512,128]{1,0:T(8,128)} %b_hbm.1, ...), custom_call_target="tpu_custom_call" | custom-call | tf_op jit(solution)/shard_map/scan_backward/pallas_call | solution.py:510
  56.2 1.3 %copy.14 = f32[512,1024]{1,0:T(8,128)} copy(f32[512,1024]{1,0:T(8,128)S(1)} %get-tuple-element.4) | data formatting | bytes 4194304
  57.5 0.6 %copy.15 = f32[16,512]{1,0:T(8,128)} copy(f32[16,512]{1,0:T(8,128)S(1)} %get-tuple-element.5) | data formatting | bytes 65536
  58.1 0.7 %copy.16 = f32[512,128]{1,0:T(8,128)} copy(f32[512,128]{1,0:T(8,128)S(1)} %get-tuple-element.6) | data formatting | bytes 524288
  58.8 0.7 %copy.17 = f32[512,128]{1,0:T(8,128)} copy(f32[512,128]{1,0:T(8,128)S(1)} %get-tuple-element.7) | data formatting | bytes 524288
